TPU v7x, 256 devices: a whole 4x4x8 slice. The times are simulated.
256 devices in a mesh: grp: 8 (over z), tok: 32 (over y, x, core).
Axes of the slice: x: 4, y: 4, z: 8, core: 2. Of those that a mesh axis runs over, the one named last changes fastest.
Arguments:
- residual_in: bfloat16 [8192, 2048], P(('tok', 'grp')), may hold values from -2.5 to 2.5
- queries: bfloat16 [8192, 2048], P('tok', 'grp'), may hold values from -120 to 120
- fresh_pairs: bfloat16 [8192, 2048], P('tok'), may hold values from -6 to 6
- cache_pairs: bfloat16 [16384, 2048], P('tok'), may hold values from -6 to 6
- segment_ids: int32 [8192], replicated, may hold values from 0 to 15, never falling along the last dimension, each value on 1 to 4096 neighbouring positions
- prefix_length: int32 [16], replicated, may hold values from 0 to 256, as said below
- page_order: int32 [1024], replicated, may hold values from 0 to 1023, each once
- out_weight: bfloat16 [2048, 2048], P('grp'), may hold values from -0.125 to 0.125
- post_gain: float32 [2048], replicated, may hold values from 0.25 to 1.75
- gate_weight: bfloat16 [2048, 4096], P(None, 'grp'), may hold values from -0.125 to 0.125
- up_weight: bfloat16 [2048, 4096], P(None, 'grp'), may hold values from -0.125 to 0.125
- down_weight: bfloat16 [4096, 2048], P('grp'), may hold values from -0.09375 to 0.09375
- next_gain: float32 [2048], replicated, may hold values from 0.25 to 1.75
- next_weight: bfloat16 [2048, 4096], P(None, 'grp'), may hold values from -0.125 to 0.125
Outputs:
- attended: bfloat16 [8192, 2048], P('tok', 'grp')
- new_cache: bfloat16 [16384, 2048], P('tok', 'grp')
- layer_out: bfloat16 [8192, 2048], P(('tok', 'grp'))
- next_proj: bfloat16 [8192, 4096], P('tok', 'grp')
Inputs may be any that keep to these rules, and one draw needn't show every extreme that they name: `segment_ids`: segment numbers never fall along the stream; each of the 16 segments has 1 to 4096 tokens and one has exactly 4096. `prefix_length`: one segment has exactly 256 cached tokens. `page_order`: each page number appears once.
All inputs are finite; a program needn't handle non-finite values.
Results may differ from a plain program's by a relative error of at most 0.024.
Values may be sent and summed in bfloat16 or wider, within the bound.
A program may use at most 128 MiB of HBM per device.

v0:
```python
import math
import jax
import jax.numpy as jnp
from jax import lax
from jax.sharding import PartitionSpec as P

HD = 256
PAGE = 16
masked_score = -1e30
norm_epsilon = 1e-05


def page_tables(segment_ids, prefix_length, page_order, page_rows):
    seg_count = prefix_length.shape[0]
    seg_range = jnp.arange(seg_count, dtype=jnp.int32)
    seg_len = jnp.sum(
        (segment_ids[None, :] == seg_range[:, None]).astype(jnp.int32), axis=1, dtype=jnp.int32
    )
    seg_start = jnp.cumsum(seg_len, dtype=jnp.int32) - seg_len
    needed = (prefix_length + seg_len + page_rows - 1) // page_rows
    cum_end = jnp.cumsum(needed, dtype=jnp.int32)
    first_slot = cum_end - needed
    page_count = page_order.shape[0]
    page_range = jnp.arange(page_count, dtype=jnp.int32)
    ranking = jnp.sum(
        jnp.where(page_order[None, :] == page_range[:, None], page_range[None, :], 0),
        axis=1,
        dtype=jnp.int32,
    )
    owners = jnp.sum(
        (cum_end[None, :] <= ranking[:, None]).astype(jnp.int32), axis=1, dtype=jnp.int32
    )
    onehot = (owners[:, None] == seg_range[None, :]).astype(jnp.int32)
    page_first = (
        ranking - jnp.sum(onehot * first_slot[None, :], axis=1, dtype=jnp.int32)
    ) * page_rows
    page_prefix = jnp.sum(onehot * prefix_length[None, :], axis=1, dtype=jnp.int32)
    page_len = jnp.sum(onehot * seg_len[None, :], axis=1, dtype=jnp.int32)
    page_start = jnp.sum(onehot * seg_start[None, :], axis=1, dtype=jnp.int32)
    return (owners, page_first, page_prefix, page_len, page_start)


def row_info(tables, row_first, count, page_rows):
    sliced = [
        jnp.repeat(
            lax.dynamic_slice_in_dim(table, row_first // page_rows, count // page_rows), page_rows
        )
        for table in tables
    ]
    position = sliced[1] + (row_first + jnp.arange(count, dtype=jnp.int32)) % page_rows
    return (sliced[0], position, sliced[2], sliced[3], sliced[4])


def attend_piece(state, query_four, pairs, visible):
    maxima, totals, weighted = state
    rows_here = pairs.shape[0]
    split = pairs.reshape(rows_here, query_four.shape[1], 2, query_four.shape[3])
    score_scale = 1.0 / math.sqrt(HD)
    scores = (
        jnp.einsum("tkgd,nkd->tkgn", query_four, split[:, :, 0], preferred_element_type=jnp.float32)
        * score_scale
    )
    live = visible[:, None, None, :]
    scores = jnp.where(live, scores, masked_score)
    raised = jnp.maximum(maxima, jnp.max(scores, axis=3))
    weights = jnp.where(live, jnp.exp(scores - raised[..., None]), 0.0)
    rescale = jnp.exp(maxima - raised)
    totals = totals * rescale + jnp.sum(weights, axis=3)
    weighted = weighted * rescale[..., None] + jnp.einsum(
        "tkgn,nkd->tkgd",
        weights.astype(jnp.bfloat16),
        split[:, :, 1],
        preferred_element_type=jnp.float32,
    )
    return (raised, totals, weighted)


def update_state(state, query_four, pairs, visible):
    return attend_piece(state, query_four, pairs, visible)


def empty_state(rows_here, pairs_here, per_pair):
    return (
        jnp.full((rows_here, pairs_here, per_pair), masked_score, jnp.float32),
        jnp.zeros((rows_here, pairs_here, per_pair), jnp.float32),
        jnp.zeros((rows_here, pairs_here, per_pair, HD), jnp.float32),
    )


def rms_scale(rows, gain):
    values = rows.astype(jnp.float32)
    scaled = values * lax.rsqrt(jnp.mean(values * values, axis=-1, keepdims=True) + norm_epsilon)
    return (scaled * gain).astype(jnp.bfloat16)


def local(
    residual_in,
    queries,
    fresh_pairs,
    cache_pairs,
    segment_ids,
    prefix_length,
    page_order,
    out_weight,
    post_gain,
    gate_weight,
    up_weight,
    down_weight,
    next_gain,
    next_weight,
):
    group = lax.axis_index("grp")
    shard = lax.axis_index("tok")
    groups = lax.axis_size("grp")
    tok_rows = queries.shape[0]
    heads_here = queries.shape[1] // HD
    pairs_here = max(1, heads_here // 2)
    per_pair = heads_here // pairs_here
    kv_first = group * heads_here // 2
    width_pairs = pairs_here * 2 * HD
    own_cols = cache_pairs.shape[1] // groups
    own_offset = group * own_cols - kv_first * 2 * HD
    query_four = queries.reshape(tok_rows, pairs_here, per_pair, HD)
    own_first = shard * tok_rows
    own_pos = own_first + jnp.arange(tok_rows, dtype=jnp.int32)
    own_seg = lax.dynamic_slice_in_dim(segment_ids, own_first, tok_rows)
    tables = page_tables(segment_ids, prefix_length, page_order, PAGE)
    cache_rows = cache_pairs.shape[0]
    cache_first = shard * cache_rows
    fresh_mine = lax.dynamic_slice_in_dim(fresh_pairs, kv_first * 2 * HD, width_pairs, 1)
    cache_mine = lax.dynamic_slice_in_dim(cache_pairs, kv_first * 2 * HD, width_pairs, 1)
    cache_info = row_info(tables, cache_first, cache_rows, PAGE)
    portion = lax.all_gather(cache_mine, "tok", axis=0, tiled=True)
    info = row_info(tables, jnp.int32(0), portion.shape[0], PAGE)
    visible = (info[0][None, :] == own_seg[:, None]) & (info[1] < info[2])[None, :]
    state = update_state(empty_state(tok_rows, pairs_here, per_pair), query_four, portion, visible)
    write_live = (cache_info[1] >= cache_info[2]) & (cache_info[1] < cache_info[2] + cache_info[3])
    write_token = cache_info[4] + cache_info[1] - cache_info[2]
    own_cache = lax.dynamic_slice_in_dim(cache_pairs, group * own_cols, own_cols, 1)
    portion = lax.all_gather(fresh_mine, "tok", axis=0, tiled=True)
    current = state
    written = own_cache
    count = portion.shape[0]
    key_pos = jnp.arange(count, dtype=jnp.int32)
    visible = (segment_ids[None, :] == own_seg[:, None]) & (key_pos[None, :] <= own_pos[:, None])
    current = update_state(current, query_four, portion, visible)
    landing = write_live & (write_token >= 0) & (write_token < count)
    mine = lax.dynamic_slice_in_dim(portion, own_offset, own_cols, 1)
    taken = jnp.take(mine, jnp.clip(write_token, 0, count - 1), axis=0)
    written = jnp.where(landing[:, None], taken, written)
    maxima, totals, weighted = current
    attended = (
        (weighted / totals[..., None]).reshape(tok_rows, heads_here * HD).astype(jnp.bfloat16)
    )
    mixed = lax.psum_scatter(
        jnp.dot(attended, out_weight, preferred_element_type=jnp.float32).astype(jnp.bfloat16),
        "grp",
        scatter_dimension=0,
        tiled=True,
    ).astype(jnp.float32)
    first_sum = (residual_in.astype(jnp.float32) + mixed).astype(jnp.bfloat16)
    post_normed = rms_scale(first_sum, post_gain)
    portion = lax.all_gather(post_normed, "grp", axis=0, tiled=True)
    gate = jnp.dot(portion, gate_weight, preferred_element_type=jnp.float32)
    up_part = jnp.dot(portion, up_weight, preferred_element_type=jnp.float32)
    hidden = (jax.nn.silu(gate) * up_part).astype(jnp.bfloat16)
    partial_rows = jnp.dot(hidden, down_weight, preferred_element_type=jnp.float32)
    ffn_out = lax.psum_scatter(
        partial_rows.astype(jnp.bfloat16), "grp", scatter_dimension=0, tiled=True
    ).astype(jnp.float32)
    layer_out = (first_sum.astype(jnp.float32) + ffn_out).astype(jnp.bfloat16)
    next_normed = rms_scale(layer_out, next_gain)
    next_proj = jnp.dot(
        lax.all_gather(next_normed, "grp", axis=0, tiled=True),
        next_weight,
        preferred_element_type=jnp.float32,
    ).astype(jnp.bfloat16)
    return (attended, written, layer_out, next_proj)


def solution(mesh):
    in_specs = (
        P(("tok", "grp"), None),
        P("tok", "grp"),
        P("tok", None),
        P("tok", None),
        P(),
        P(),
        P(),
        P("grp", None),
        P(),
        P(None, "grp"),
        P(None, "grp"),
        P("grp", None),
        P(),
        P(None, "grp"),
    )
    out_specs = (P("tok", "grp"), P("tok", "grp"), P(("tok", "grp"), None), P("tok", "grp"))
    return jax.shard_map(local, mesh=mesh, in_specs=in_specs, out_specs=out_specs, check_vma=False)
```

profile of v0, /device:TPU:2, one launch (start us, length us, event | category | flops | bytes accessed | tf_op | source)
XLA Modules:
  0.0 377.0 jit_solution(1616883388557246644)
XLA Ops:
  7.2 1.8 constant_dynamic-slice_fusion.1
  9.1 0.0 all-gather.5.cloned.1.call-start
  9.1 1.1 constant_dynamic-slice_fusion.2
  10.2 1.0 copy.42
  11.3 0.0 reduce-scatter.3.cloned.1.call-start
  11.3 0.8 dynamic_slice.30
  12.1 0.9 convert_reduce_fusion
  13.0 0.1 copy.40
  13.1 0.1 reduce.5
  13.3 0.7 fusion.79
  13.9 0.1 copy.34
  14.1 0.1 reduce.4
  14.2 1.2 select_reduce_fusion
  15.4 0.1 convert_reduce_fusion.1
  15.5 1.4 select_reduce_fusion.2
  16.9 0.2 broadcast_in_dim.108
  17.1 0.2 reshape.509
  17.3 0.2 broadcast_in_dim.107
  17.5 0.2 reshape.508
  17.7 0.2 broadcast_in_dim.106
  17.9 0.2 eq.89
  18.1 53.8 %all-gather.7.cloned.1.call-done = bf16[8192,512]{1,0:T(8,128)(2,1)} async-done(((bf16[256,512]{1,0:T(8,128)(2,1)}), bf16[8192,512]{1,0:T(8,128)(2,1)}) %all-gather.7.cloned.1.call-update) | async-done | bytes 8388624 | tf_op jit(solution)/shard_map/all_gather | solution.py:140
  71.9 12.5 %reshape.514 = bf16[8192,1,2,256]{3,2,0,1:T(2,128)(2,1)} reshape(bf16[8192,512]{1,0:T(8,128)(2,1)} %all-gather.7.cloned.1.call-done) | data formatting | bytes 16777216 | tf_op jit(solution)/shard_map/reshape | solution.py:57
  84.4 17.2 %fusion.78 = (bf16[8192,1,1,256]{3,2,0,1:T(2,128)(2,1)}, bf16[8192,1,1,256]{3,2,0,1:T(2,128)(2,1)S(1)}) fusion(bf16[8192,1,2,256]{3,2,0,1:T(2,128)(2,1)} %reshape.514), kind=kLoop, calls=%fused_computation.121 | loop fusion | bytes 16777216 | tf_op jit(solution)/shard_map/slice | solution.py:72
  101.6 7.7 %fusion.81 = (f32[256]{0:T(256)S(1)}, f32[256,1,1,8192]{0,3,2,1:T(8,128)}) fusion(bf16[256,256]{1,0:T(8,128)(2,1)S(1)} %copy-done.9, bf16[8192,1,1,256]{3,2,0,1:T(2,128)(2,1)S(1)} %get-tuple-element.29, s32[256]{0:T(256)S(1)} %iota_add_fusion, s32[256]{0:T(256)S(1)} %dynamic_slice.30, s32[8192]{0:T(1024)S(1)} %copy-done.6), kind=kOutput, calls=%fused_computation.124 | convolution fusion | flops 1086324480 | bytes 12749824 | tf_op jit(solution)/shard_map/tkgd,nkd->tkgn/dot_general | solution.py:60
  109.3 49.4 %all-gather.5.cloned.1.call-done = bf16[16384,512]{0,1:T(8,128)(2,1)} async-done(((bf16[512,512]{0,1:T(8,128)(2,1)}), bf16[16384,512]{0,1:T(8,128)(2,1)}) %all-gather.5.cloned.1.call-update) | async-done | bytes 16777232 | tf_op jit(solution)/shard_map/all_gather | solution.py:133
  158.7 9.8 %fusion.80 = (f32[256]{0:T(256)S(1)}, f32[256,1,1,16384]{0,3,2,1:T(8,128)S(1)}) fusion(bf16[256,256]{1,0:T(8,128)(2,1)S(1)} %copy-done.9, bf16[16384,1,2,256]{0,3,2,1:T(8,128)(2,1)} %bitcast.108, pred[16384]{0:T(1024)(128)(4,1)S(1)} %fusion.62, s32[256]{0:T(256)S(1)} %dynamic_slice.30, s32[16384]{0:T(1024)S(1)} %eq.89), kind=kOutput, calls=%fused_computation.123 | convolution fusion | flops 2168454912 | bytes 25380864 | tf_op jit(solution)/shard_map/tkgd,nkd->tkgn/dot_general | solution.py:60
  168.5 3.9 %fusion.14 = f32[256]{0:T(256)S(1)} fusion(f32[256,1,1,8192]{0,3,2,1:T(8,128)S(1)} %copy-done.1, f32[256]{0:T(256)S(1)} %get-tuple-element.33, s32[256]{0:T(256)S(1)} %iota_add_fusion, s32[256]{0:T(256)S(1)} %dynamic_slice.30, s32[8192]{0:T(1024)S(1)} %copy-done.6), kind=kLoop, calls=%fused_computation.22 | loop fusion | flops 12582656 | bytes 8425472 | tf_op jit(solution)/shard_map/reduce_sum | solution.py:68
  172.4 3.2 fusion.24
  175.7 6.0 %fusion.2 = f32[256]{0:T(256)S(1)} fusion(f32[256,1,1,16384]{0,3,2,1:T(8,128)S(1)} %get-tuple-element.38, f32[256]{0:T(256)S(1)} %get-tuple-element.34, s32[256]{0:T(256)S(1)} %dynamic_slice.30, s32[16384]{0:T(1024)S(1)} %eq.89, pred[16384]{0:T(1024)(128)(4,1)S(1)} %fusion.62), kind=kLoop, calls=%fused_computation.6 | loop fusion | flops 20971264 | bytes 16862208 | tf_op jit(solution)/shard_map/reduce_sum | solution.py:68
  181.7 20.1 %fusion.45 = bf16[256,256]{0,1:T(8,128)(2,1)S(1)} fusion(f32[1,256,256,1]{2,1,3,0:T(8,128)S(1)} %fusion.24, f32[256,1,1,16384]{0,3,2,1:T(8,128)S(1)} %get-tuple-element.38, f32[256]{0:T(256)S(1)} %get-tuple-element.34, s32[256]{0:T(256)S(1)} %dynamic_slice.30, s32[16384]{0:T(1024)S(1)} %eq.89, pred[16384]{0:T(1024)(128)(4,1)S(1)} %fusion.62, ...), kind=kOutput, calls=%fused_computation.46 | convolution fusion | flops 2168782848 | bytes 25646080 | tf_op jit(solution)/shard_map/tkgn,nkd->tkgd/dot_general | solution.py:69
  201.8 1.5 convolution_convert_fusion.1
  203.3 0.0 all-gather.9.cloned.1.call-start
  203.3 39.7 %reduce-scatter.3.cloned.1.call-done = bf16[32,2048]{1,0:T(8,128)(2,1)} async-done(((bf16[256,2048]{1,0:T(8,128)(2,1)}), bf16[32,2048]{1,0:T(8,128)(2,1)}) %reduce-scatter.3.cloned.1.call-update) | async-done | bytes 131088 | tf_op jit(solution)/shard_map/reduce_scatter | solution.py:155
  243.0 1.1 fusion.56
  244.1 1.7 fusion.58
  245.8 0.2 reduce-scatter.5.cloned.1.call-start
  246.0 37.0 %all-gather.9.cloned.1.call-done = bf16[256,2048]{1,0:T(8,128)(2,1)} async-done(((bf16[32,2048]{1,0:T(8,128)(2,1)}), bf16[256,2048]{1,0:T(8,128)(2,1)}) %all-gather.9.cloned.1.call-update) | async-done | bytes 1048592 | tf_op jit(solution)/shard_map/all_gather | solution.py:163
  283.0 2.6 fusion.82
  285.6 4.3 %convolution_convert_fusion = bf16[256,2048]{1,0:T(8,128)(2,1)} fusion(bf16[512,2048]{1,0:T(8,128)(2,1)S(1)} %copy-done, bf16[256,2048]{1,0:T(8,128)(2,1)} %all-gather.9.cloned.1.call-done, bf16[2048,512]{1,0:T(8,128)(2,1)} %param.24, f32[256,512]{1,0:T(8,128)S(1)} %fusion.82), kind=kOutput, calls=%fused_computation.34 | convolution fusion | flops 1075052544 | bytes 6815744 | tf_op jit(solution)/shard_map/dot_general | solution.py:167
  290.0 37.5 %reduce-scatter.5.cloned.1.call-done = bf16[32,2048]{1,0:T(8,128)(2,1)} async-done(((bf16[256,2048]{1,0:T(8,128)(2,1)}), bf16[32,2048]{1,0:T(8,128)(2,1)}) %reduce-scatter.5.cloned.1.call-update) | async-done | bytes 131088 | tf_op jit(solution)/shard_map/reduce_scatter | solution.py:168
  327.5 1.1 fusion.53
  328.6 0.8 fusion.55
  329.4 0.1 dynamic_slice.33
  329.5 0.1 dynamic_slice.34
  329.6 0.1 broadcast_in_dim.115
  329.6 0.1 reshape.526
  329.7 0.1 reshape.519
  329.8 0.1 dynamic_slice.36
  329.9 0.1 broadcast_in_dim.117
  329.9 0.1 reshape.524
  330.0 0.1 reshape.523
  330.1 0.1 broadcast_in_dim.114
  330.2 0.1 reshape.525
  330.3 0.1 reshape.518
  330.3 0.1 dynamic_slice.35
  330.4 0.1 broadcast_in_dim.116
  330.5 0.1 reshape.520
  330.7 4.4 %constant_dynamic-slice_fusion = bf16[8192,256]{1,0:T(8,128)(2,1)} fusion(bf16[8192,512]{1,0:T(8,128)(2,1)} %all-gather.7.cloned.1.call-done, s32[]{:T(128)S(6)} %select_n.127), kind=kLoop, calls=%fused_computation.111 | loop fusion | bytes 8388612 | tf_op jit(solution)/shard_map/dynamic_slice | solution.py:148
  335.0 4.3 %gather_fusion = bf16[512,256]{1,0:T(8,128)(2,1)S(1)} fusion(bf16[8192,256]{1,0:T(8,128)(2,1)} %constant_dynamic-slice_fusion, s32[1024]{0:T(1024)S(1)} %pad_clamp_fusion), kind=kCustom, calls=%fused_computation | custom fusion | bytes 526336 | tf_op jit(solution)/shard_map/jit(_take)/gather | solution.py:149
  339.3 1.9 dynamic-slice_select_fusion
  341.2 0.8 copy.41
  342.0 24.9 %all-gather.11.cloned.1.call-done = bf16[256,2048]{1,0:T(8,128)(2,1)} async-done(((bf16[32,2048]{1,0:T(8,128)(2,1)}), bf16[256,2048]{1,0:T(8,128)(2,1)}) %all-gather.11.cloned.1.call-update) | async-done | bytes 1048592 | tf_op jit(solution)/shard_map/all_gather | solution.py:174
  366.8 3.3 convolution_convert_fusion.2
  (46 shorter events, 0.4 us)
Async XLA Ops:
  7.2 278.5 %copy-start = (bf16[512,2048]{1,0:T(8,128)(2,1)S(1)}, bf16[512,2048]{1,0:T(8,128)(2,1)}, u32[]{:S(2)}) copy-start(bf16[512,2048]{1,0:T(8,128)(2,1)} %param.25) | copy-start | bytes 6291460
  7.2 64.7 %all-gather.7.cloned.1.call-start = ((), (), s32[]{:S(2)}) async-start(), calls=%async_computation.3 | async-start | bytes 8650752 | tf_op jit(solution)/shard_map/all_gather | solution.py:140
  9.1 149.6 %all-gather.5.cloned.1.call-start = ((), (), s32[]{:S(2)}) async-start(), calls=%async_computation.2 | async-start | bytes 17301504 | tf_op jit(solution)/shard_map/all_gather | solution.py:133
  11.3 231.7 %reduce-scatter.3.cloned.1.call-start = ((), (), s32[]{:S(2)}) async-start(), calls=%async_computation.4 | async-start | bytes 1179648 | tf_op jit(solution)/shard_map/reduce_scatter | solution.py:155
  84.4 17.2 %copy-start.6 = (s32[8192]{0:T(1024)S(1)}, s32[8192]{0:T(1024)}, u32[]{:S(2)}) copy-start(s32[8192]{0:T(1024)} %param.18) | copy-start | bytes 98308
  84.4 17.2 %copy-start.9 = (bf16[256,256]{1,0:T(8,128)(2,1)S(1)}, bf16[256,256]{1,0:T(8,128)(2,1)}, u32[]{:S(2)}) copy-start(bf16[256,256]{1,0:T(8,128)(2,1)} %param.15) | copy-start | bytes 393220
  158.7 13.7 %slice-start = ((s8[8388608]{0:T(1024)(128)(4,1)}), s8[4194304]{0:T(1024)(128)(4,1)S(1)}, s32[]{:S(2)}) async-start(s8[8388608]{0:T(1024)(128)(4,1)} %bitcast.103), calls=%async_computation.8 | async-start | bytes 8388608
  158.7 9.8 %copy-start.1 = (f32[256,1,1,8192]{0,3,2,1:T(8,128)S(1)}, f32[256,1,1,8192]{0,3,2,1:T(8,128)}, u32[]{:S(2)}) copy-start(f32[256,1,1,8192]{0,3,2,1:T(8,128)} %get-tuple-element.40) | copy-start | bytes 25165828
  158.7 13.7 %slice-start.1 = ((s8[8388608]{0:T(1024)(128)(4,1)}), s8[4194304]{0:T(1024)(128)(4,1)S(1)}, s32[]{:S(2)}) async-start(s8[8388608]{0:T(1024)(128)(4,1)} %bitcast.103), calls=%async_computation.9 | async-start | bytes 8388608
  181.6 20.1 %copy-start.4 = (bf16[256,2048]{1,0:T(8,128)(2,1)S(1)}, bf16[256,2048]{1,0:T(8,128)(2,1)}, u32[]{:S(2)}) copy-start(bf16[256,2048]{1,0:T(8,128)(2,1)} %param.21) | copy-start | bytes 3145732
  181.7 61.3 %copy-start.2 = (bf16[32,2048]{1,0:T(8,128)(2,1)S(1)}, bf16[32,2048]{1,0:T(8,128)(2,1)}, u32[]{:S(2)}) copy-start(bf16[32,2048]{1,0:T(8,128)(2,1)} %param.14) | copy-start | bytes 393220
  181.7 62.5 %copy-start.7 = (f32[2048]{0:T(1024)S(1)}, f32[2048]{0:T(1024)}, u32[]{:S(2)}) copy-start(f32[2048]{0:T(1024)} %param.22) | copy-start | bytes 24580
  203.2 125.4 %copy-start.8 = (f32[2048]{0:T(1024)S(1)}, f32[2048]{0:T(1024)}, u32[]{:S(2)}) copy-start(f32[2048]{0:T(1024)} %param.26) | copy-start | bytes 24580
  203.3 79.7 %all-gather.9.cloned.1.call-start = ((), (), s32[]{:S(2)}) async-start(), calls=%async_computation.5 | async-start | bytes 1179648 | tf_op jit(solution)/shard_map/all_gather | solution.py:163
  243.0 84.5 %copy-start.3 = (bf16[32,2048]{1,0:T(8,128)(2,1)S(1)}, bf16[32,2048]{1,0:T(8,128)(2,1)}, u32[]{:S(2)}) copy-start(bf16[32,2048]{1,0:T(8,128)(2,1)} %reduce-scatter.3.cloned.1.call-done) | copy-start | bytes 393220
  245.8 81.7 %reduce-scatter.5.cloned.1.call-start = ((), (), s32[]{:S(2)}) async-start(), calls=%async_computation.6 | async-start | bytes 1179648 | tf_op jit(solution)/shard_map/reduce_scatter | solution.py:168
  289.9 76.9 %all-gather.11.cloned.1.call-start = ((), (), s32[]{:S(2)}) async-start(), calls=%async_computation.7 | async-start | bytes 1179648 | tf_op jit(solution)/shard_map/all_gather | solution.py:174
  328.6 41.6 %copy-start.5 = (bf16[32,2048]{1,0:T(8,128)(2,1)}, bf16[32,2048]{1,0:T(8,128)(2,1)S(1)}, u32[]{:S(2)}) copy-start(bf16[32,2048]{1,0:T(8,128)(2,1)S(1)} %get-tuple-element.25) | copy-start | bytes 393220
Sparse Core Ops, SparseCore 0:
  11.1 60.7 all-gather.6
  74.4 84.2 all-gather.4
  203.4 39.5 reduce-scatter.2
  245.9 37.0 all-gather.8
  290.1 37.3 reduce-scatter.4
  329.7 37.0 all-gather.10
where the time goes:
time: 378 us; the launch traced here: 377 us
  waiting for transfers between devices  242 us (64%)
  matrix products  52.4 us (14%)
  local copies, waits for them, and re-layouts  46.4 us (12%)
  other arithmetic  21.1 us (6%)
  between operations  14.5 us (4%)
    all_gather x1, waiting for transfers between devices, local(): portion = lax.all_gather(fresh_mine, 'tok', axis=0, tiled=True)  53.8 us
    all_gather x1, waiting for transfers between devices, local(): portion = lax.all_gather(cache_mine, 'tok', axis=0, tiled=True)  49.4 us
    reduce_scatter x1, waiting for transfers between devices, local(): lax.psum_scatter(jnp.dot(attended, out_weight, preferred_element_type=jnp...  39.7 us
    reduce_scatter x1, waiting for transfers between devices, local(): lax.psum_scatter(partial_rows.astype(jnp.bfloat16), 'grp', scatter_dimens...  37.5 us
    all_gather x1, waiting for transfers between devices, local(): portion = lax.all_gather(post_normed, 'grp', axis=0, tiled=True)  37 us
    all_gather x1, waiting for transfers between devices, local(): lax.all_gather(next_normed, 'grp', axis=0, tiled=True)  24.9 us
    dot_general x2, matrix products, attend_piece(): jnp.einsum('tkgn,nkd->tkgd', weights.astype(jnp.bfloat16), split[:, :, 1]...  23.3 us
    dot_general x2, matrix products, attend_piece(): jnp.einsum('tkgd,nkd->tkgn', query_four, split[:, :, 0], preferred_elemen...  17.5 us
  transfers between devices with their start and end apart: 6, of which 6 were waited for; matrix products, arithmetic and copies ran while one was open for 16% of the time, Pallas kernels for 0%

commit v1 on v0

--- a/solution.py
+++ b/solution.py
@@ -8,6 +8,22 @@
 PAGE = 16
 masked_score = -1e30
 norm_epsilon = 1e-05
+
+
+def gather_around(x, axis, dim):
+    ways, here, lap = (lax.axis_size(axis), lax.axis_index(axis), x.shape[dim])
+    dims = [n * ways if d == dim else n for d, n in enumerate(x.shape)]
+    full = lax.dynamic_update_slice_in_dim(jnp.zeros(dims, x.dtype), x, here * lap, axis=dim)
+    going_up = going_down = x
+    for far in range(1, ways // 2 + 1):
+        going_up = lax.ppermute(going_up, axis, [(d, (d + 1) % ways) for d in range(ways)])
+        full = lax.dynamic_update_slice_in_dim(full, going_up, (here - far) % ways * lap, axis=dim)
+        if 2 * far < ways:
+            going_down = lax.ppermute(going_down, axis, [(d, (d - 1) % ways) for d in range(ways)])
+            full = lax.dynamic_update_slice_in_dim(
+                full, going_down, (here + far) % ways * lap, axis=dim
+            )
+    return full
 
 
 def page_tables(segment_ids, prefix_length, page_order, page_rows):
@@ -171,9 +187,7 @@
     layer_out = (first_sum.astype(jnp.float32) + ffn_out).astype(jnp.bfloat16)
     next_normed = rms_scale(layer_out, next_gain)
     next_proj = jnp.dot(
-        lax.all_gather(next_normed, "grp", axis=0, tiled=True),
-        next_weight,
-        preferred_element_type=jnp.float32,
+        gather_around(next_normed, "grp", 0), next_weight, preferred_element_type=jnp.float32
     ).astype(jnp.bfloat16)
     return (attended, written, layer_out, next_proj)
 

time: 378 us -> 367 us (0.971)
  waiting for transfers between devices: 242 us -> 218 us
  starting transfers between devices: 0.43 us -> 10.6 us
  local copies, waits for them, and re-layouts: 46.4 us -> 50.3 us
    all_gather x1 -> x0, waiting for transfers between devices: 24.9 us -> none  [local(): lax.all_gather(next_normed, 'grp', axis=0, tiled=True)]
    ppermute x0 -> x7, waiting for transfers between devices: none -> 10.8 us  [the longest x4 10.8 us: gather_around(): lax.ppermute(going_up, axis, [(d, (d + 1) % ways) for d in range(ways)])]
    ppermute x0 -> x7, starting transfers between devices: none -> 10.3 us  [the longest x3 9.34 us: gather_around(): lax.ppermute(going_down, axis, [(d, (d - 1) % ways) for d in range(ways)])]
    reduce_scatter x1, waiting for transfers between devices: 37.5 us -> 27.4 us  [local(): lax.psum_scatter(partial_rows.astype(jnp.bfloat16), 'grp', scatter_dimens...]
  transfers between devices with their start and end apart: 6 -> 12, of which waited for: 6 -> 9; matrix products, arithmetic and copies ran while one was open for 16% -> 17% of each run, Pallas kernels for 0% -> 0%
where the time goes in v1:
time: 367 us; the launch traced here: 366 us
  waiting for transfers between devices  218 us (59%)
  matrix products  52.1 us (14%)
  local copies, waits for them, and re-layouts  50.3 us (14%)
  other arithmetic  20.3 us (6%)
  between operations  14.3 us (4%)
  starting transfers between devices  10.6 us (3%)
    all_gather x1, waiting for transfers between devices, local(): portion = lax.all_gather(fresh_mine, 'tok', axis=0, tiled=True)  53.8 us
    all_gather x1, waiting for transfers between devices, local(): portion = lax.all_gather(cache_mine, 'tok', axis=0, tiled=True)  49.4 us
    reduce_scatter x1, waiting for transfers between devices, local(): lax.psum_scatter(jnp.dot(attended, out_weight, preferred_element_type=jnp...  39.7 us
    all_gather x1, waiting for transfers between devices, local(): portion = lax.all_gather(post_normed, 'grp', axis=0, tiled=True)  37 us
    reduce_scatter x1, waiting for transfers between devices, local(): lax.psum_scatter(partial_rows.astype(jnp.bfloat16), 'grp', scatter_dimens...  27.4 us
    dot_general x2, matrix products, attend_piece(): jnp.einsum('tkgn,nkd->tkgd', weights.astype(jnp.bfloat16), split[:, :, 1]...  23.3 us
    dot_general x2, matrix products, attend_piece(): jnp.einsum('tkgd,nkd->tkgn', query_four, split[:, :, 0], preferred_elemen...  17.4 us
    slice x1, local copies, waits for them, and re-layouts, attend_piece(): split[:, :, 1]  17.2 us
  transfers between devices with their start and end apart: 12, of which 9 were waited for; matrix products, arithmetic and copies ran while one was open for 17% of the time, Pallas kernels for 0%

profile of v1, /device:TPU:2, one launch (start us, length us, event | category | flops | bytes accessed | tf_op | source)
XLA Modules:
  0.0 365.8 jit_solution(9299596596377045157)
XLA Ops:
  7.2 1.8 constant_dynamic-slice_fusion.1
  9.1 1.1 constant_dynamic-slice_fusion.2
  10.2 1.0 copy.42
  11.3 0.8 dynamic_slice.30
  12.1 0.9 convert_reduce_fusion
  13.0 0.1 copy.40
  13.1 0.1 reduce.5
  13.3 0.7 fusion.80
  13.9 0.1 copy.34
  14.1 0.1 reduce.4
  14.2 1.2 select_reduce_fusion
  15.4 0.1 convert_reduce_fusion.1
  15.5 1.4 select_reduce_fusion.2
  16.9 0.2 broadcast_in_dim.111
  17.1 0.2 reshape.509
  17.3 0.2 broadcast_in_dim.110
  17.5 0.2 reshape.508
  17.7 0.2 broadcast_in_dim.109
  17.9 0.2 eq.97
  18.1 53.8 %all-gather.6.cloned.1.call-done = bf16[8192,512]{1,0:T(8,128)(2,1)} async-done(((bf16[256,512]{1,0:T(8,128)(2,1)}), bf16[8192,512]{1,0:T(8,128)(2,1)}) %all-gather.6.cloned.1.call-update) | async-done | bytes 8388624 | tf_op jit(solution)/shard_map/all_gather | solution.py:156
  71.9 12.5 %reshape.514 = bf16[8192,1,2,256]{3,2,0,1:T(2,128)(2,1)} reshape(bf16[8192,512]{1,0:T(8,128)(2,1)} %all-gather.6.cloned.1.call-done) | data formatting | bytes 16777216 | tf_op jit(solution)/shard_map/reshape | solution.py:73
  84.4 17.2 %fusion.79 = (bf16[8192,1,1,256]{3,2,0,1:T(2,128)(2,1)}, bf16[8192,1,1,256]{3,2,0,1:T(2,128)(2,1)S(1)}) fusion(bf16[8192,1,2,256]{3,2,0,1:T(2,128)(2,1)} %reshape.514), kind=kLoop, calls=%fused_computation.129 | loop fusion | bytes 16777216 | tf_op jit(solution)/shard_map/slice | solution.py:88
  101.6 7.7 %fusion.82 = (f32[256]{0:T(256)S(1)}, f32[256,1,1,8192]{0,3,2,1:T(8,128)}) fusion(bf16[256,256]{1,0:T(8,128)(2,1)S(1)} %copy-done.10, bf16[8192,1,1,256]{3,2,0,1:T(2,128)(2,1)S(1)} %get-tuple-element.31, s32[256]{0:T(256)S(1)} %iota_add_fusion, s32[256]{0:T(256)S(1)} %dynamic_slice.30, s32[8192]{0:T(1024)S(1)} %copy-done.7), kind=kOutput, calls=%fused_computation.132 | convolution fusion | flops 1086324480 | bytes 12749824 | tf_op jit(solution)/shard_map/tkgd,nkd->tkgn/dot_general | solution.py:76
  109.3 49.4 %all-gather.4.cloned.1.call-done = bf16[16384,512]{0,1:T(8,128)(2,1)} async-done(((bf16[512,512]{0,1:T(8,128)(2,1)}), bf16[16384,512]{0,1:T(8,128)(2,1)}) %all-gather.4.cloned.1.call-update) | async-done | bytes 16777232 | tf_op jit(solution)/shard_map/all_gather | solution.py:149
  158.7 9.7 %fusion.81 = (f32[256]{0:T(256)S(1)}, f32[256,1,1,16384]{0,3,2,1:T(8,128)S(1)}) fusion(bf16[256,256]{1,0:T(8,128)(2,1)S(1)} %copy-done.10, bf16[16384,1,2,256]{0,3,2,1:T(8,128)(2,1)} %bitcast.108, pred[16384]{0:T(1024)(128)(4,1)S(1)} %fusion.62, s32[256]{0:T(256)S(1)} %dynamic_slice.30, s32[16384]{0:T(1024)S(1)} %eq.97), kind=kOutput, calls=%fused_computation.131 | convolution fusion | flops 2168454912 | bytes 25380864 | tf_op jit(solution)/shard_map/tkgd,nkd->tkgn/dot_general | solution.py:76
  168.5 3.9 %fusion.14 = f32[256]{0:T(256)S(1)} fusion(f32[256,1,1,8192]{0,3,2,1:T(8,128)S(1)} %copy-done.1, f32[256]{0:T(256)S(1)} %get-tuple-element.35, s32[256]{0:T(256)S(1)} %iota_add_fusion, s32[256]{0:T(256)S(1)} %dynamic_slice.30, s32[8192]{0:T(1024)S(1)} %copy-done.7), kind=kLoop, calls=%fused_computation.22 | loop fusion | flops 12582656 | bytes 8425472 | tf_op jit(solution)/shard_map/reduce_sum | solution.py:84
  172.4 3.2 fusion.24
  175.6 6.0 %fusion.2 = f32[256]{0:T(256)S(1)} fusion(f32[256,1,1,16384]{0,3,2,1:T(8,128)S(1)} %get-tuple-element.40, f32[256]{0:T(256)S(1)} %get-tuple-element.36, s32[256]{0:T(256)S(1)} %dynamic_slice.30, s32[16384]{0:T(1024)S(1)} %eq.97, pred[16384]{0:T(1024)(128)(4,1)S(1)} %fusion.62), kind=kLoop, calls=%fused_computation.6 | loop fusion | flops 20971264 | bytes 16862208 | tf_op jit(solution)/shard_map/reduce_sum | solution.py:84
  181.6 20.1 %fusion.45 = bf16[256,256]{0,1:T(8,128)(2,1)S(1)} fusion(f32[1,256,256,1]{2,1,3,0:T(8,128)S(1)} %fusion.24, f32[256,1,1,16384]{0,3,2,1:T(8,128)S(1)} %get-tuple-element.40, f32[256]{0:T(256)S(1)} %get-tuple-element.36, s32[256]{0:T(256)S(1)} %dynamic_slice.30, s32[16384]{0:T(1024)S(1)} %eq.97, pred[16384]{0:T(1024)(128)(4,1)S(1)} %fusion.62, ...), kind=kOutput, calls=%fused_computation.46 | convolution fusion | flops 2168782848 | bytes 25646080 | tf_op jit(solution)/shard_map/tkgn,nkd->tkgd/dot_general | solution.py:85
  201.7 0.6 copy-done.6
  202.4 1.4 convolution_convert_fusion.1
  203.9 39.7 %reduce-scatter.3.cloned.1.call-done = bf16[32,2048]{1,0:T(8,128)(2,1)} async-done(((bf16[256,2048]{1,0:T(8,128)(2,1)}), bf16[32,2048]{1,0:T(8,128)(2,1)}) %reduce-scatter.3.cloned.1.call-update) | async-done | bytes 131088 | tf_op jit(solution)/shard_map/reduce_scatter | solution.py:171
  243.6 1.1 fusion.56
  244.7 1.7 fusion.58
  246.4 0.2 reduce-scatter.5.cloned.1.call-start
  246.6 37.0 %all-gather.8.cloned.1.call-done = bf16[256,2048]{1,0:T(8,128)(2,1)} async-done(((bf16[32,2048]{1,0:T(8,128)(2,1)}), bf16[256,2048]{1,0:T(8,128)(2,1)}) %all-gather.8.cloned.1.call-update) | async-done | bytes 1048592 | tf_op jit(solution)/shard_map/all_gather | solution.py:179
  283.6 2.6 fusion.83
  286.2 4.3 %convolution_convert_fusion = bf16[256,2048]{1,0:T(8,128)(2,1)} fusion(bf16[512,2048]{1,0:T(8,128)(2,1)S(1)} %copy-done, bf16[256,2048]{1,0:T(8,128)(2,1)} %all-gather.8.cloned.1.call-done, bf16[2048,512]{1,0:T(8,128)(2,1)} %param.24, f32[256,512]{1,0:T(8,128)S(1)} %fusion.83), kind=kOutput, calls=%fused_computation.34 | convolution fusion | flops 1075052544 | bytes 6815744 | tf_op jit(solution)/shard_map/dot_general | solution.py:183
  290.9 0.1 reshape.526
  291.2 0.1 reshape.524
  291.3 0.1 reshape.523
  291.5 0.1 reshape.525
  291.6 0.1 reshape.518
  291.8 0.1 reshape.520
  292.0 4.4 %constant_dynamic-slice_fusion = bf16[8192,256]{1,0:T(8,128)(2,1)} fusion(bf16[8192,512]{1,0:T(8,128)(2,1)} %all-gather.6.cloned.1.call-done, s32[]{:T(128)S(6)} %select_n.181), kind=kLoop, calls=%fused_computation.100 | loop fusion | bytes 8388612 | tf_op jit(solution)/shard_map/dynamic_slice | solution.py:164
  296.3 4.3 %gather_fusion = bf16[512,256]{1,0:T(8,128)(2,1)S(1)} fusion(bf16[8192,256]{1,0:T(8,128)(2,1)} %constant_dynamic-slice_fusion, s32[1024]{0:T(1024)S(1)} %pad_clamp_fusion), kind=kCustom, calls=%fused_computation | custom fusion | bytes 526336 | tf_op jit(solution)/shard_map/jit(_take)/gather | solution.py:165
  300.6 27.4 %reduce-scatter.5.cloned.1.call-done = bf16[32,2048]{1,0:T(8,128)(2,1)} async-done(((bf16[256,2048]{1,0:T(8,128)(2,1)}), bf16[32,2048]{1,0:T(8,128)(2,1)}) %reduce-scatter.5.cloned.1.call-update) | async-done | bytes 131088 | tf_op jit(solution)/shard_map/reduce_scatter | solution.py:184
  328.1 1.1 fusion.53
  329.2 0.1 broadcast_in_dim.124
  329.3 0.1 constant_dynamic-update-slice_fusion.7
  329.4 0.4 copy-done.5
  329.8 0.9 collective-permute-start
  330.7 2.3 collective-permute-start.1
  333.0 1.9 dynamic-slice_select_fusion
  334.9 1.7 copy.41
  336.6 0.6 collective-permute-done
  337.2 3.5 collective-permute-start.3
  340.7 0.9 constant_dynamic-update-slice_fusion.6
  341.6 0.9 constant_dynamic-update-slice_fusion.5
  342.5 1.4 collective-permute-done.2
  343.9 3.5 collective-permute-start.5
  347.5 2.6 collective-permute-done.4
  350.1 6.1 %collective-permute-done.6 = bf16[32,2048]{1,0:T(8,128)(2,1)S(1)} collective-permute-done((bf16[32,2048]{1,0:T(8,128)(2,1)S(1)}, bf16[32,2048]{1,0:T(8,128)(2,1)S(1)}, u32[]{:S(2)}, u32[]{:S(2)}) %collective-permute-start.6) | collective-permute-done | bytes 131104 | tf_op jit(solution)/shard_map/ppermute | solution.py:19
  356.3 3.0 convolution_convert_fusion.2
  (67 shorter events, 1.3 us)
Async XLA Ops:
  7.2 279.0 %copy-start = (bf16[512,2048]{1,0:T(8,128)(2,1)S(1)}, bf16[512,2048]{1,0:T(8,128)(2,1)}, u32[]{:S(2)}) copy-start(bf16[512,2048]{1,0:T(8,128)(2,1)} %param.25) | copy-start | bytes 6291460
  7.2 64.7 %all-gather.6.cloned.1.call-start = ((), (), s32[]{:S(2)}) async-start(), calls=%async_computation.3 | async-start | bytes 8650752 | tf_op jit(solution)/shard_map/all_gather | solution.py:156
  9.1 149.6 %all-gather.4.cloned.1.call-start = ((), (), s32[]{:S(2)}) async-start(), calls=%async_computation.2 | async-start | bytes 17301504 | tf_op jit(solution)/shard_map/all_gather | solution.py:149
  11.3 232.4 %reduce-scatter.3.cloned.1.call-start = ((), (), s32[]{:S(2)}) async-start(), calls=%async_computation.4 | async-start | bytes 1179648 | tf_op jit(solution)/shard_map/reduce_scatter | solution.py:171
  84.4 17.2 %copy-start.7 = (s32[8192]{0:T(1024)S(1)}, s32[8192]{0:T(1024)}, u32[]{:S(2)}) copy-start(s32[8192]{0:T(1024)} %param.18) | copy-start | bytes 98308
  84.4 17.2 %copy-start.10 = (bf16[256,256]{1,0:T(8,128)(2,1)S(1)}, bf16[256,256]{1,0:T(8,128)(2,1)}, u32[]{:S(2)}) copy-start(bf16[256,256]{1,0:T(8,128)(2,1)} %param.15) | copy-start | bytes 393220
  158.7 13.7 %slice-start = ((s8[8388608]{0:T(1024)(128)(4,1)}), s8[4194304]{0:T(1024)(128)(4,1)S(1)}, s32[]{:S(2)}) async-start(s8[8388608]{0:T(1024)(128)(4,1)} %bitcast.103), calls=%async_computation.7 | async-start | bytes 8388608
  158.7 9.8 %copy-start.1 = (f32[256,1,1,8192]{0,3,2,1:T(8,128)S(1)}, f32[256,1,1,8192]{0,3,2,1:T(8,128)}, u32[]{:S(2)}) copy-start(f32[256,1,1,8192]{0,3,2,1:T(8,128)} %get-tuple-element.42) | copy-start | bytes 25165828
  158.7 13.7 %slice-start.1 = ((s8[8388608]{0:T(1024)(128)(4,1)}), s8[4194304]{0:T(1024)(128)(4,1)S(1)}, s32[]{:S(2)}) async-start(s8[8388608]{0:T(1024)(128)(4,1)} %bitcast.103), calls=%async_computation.8 | async-start | bytes 8388608
  181.6 20.8 %copy-start.4 = (bf16[256,2048]{1,0:T(8,128)(2,1)S(1)}, bf16[256,2048]{1,0:T(8,128)(2,1)}, u32[]{:S(2)}) copy-start(bf16[256,2048]{1,0:T(8,128)(2,1)} %param.21) | copy-start | bytes 3145732
  181.6 62.0 %copy-start.2 = (bf16[32,2048]{1,0:T(8,128)(2,1)S(1)}, bf16[32,2048]{1,0:T(8,128)(2,1)}, u32[]{:S(2)}) copy-start(bf16[32,2048]{1,0:T(8,128)(2,1)} %param.14) | copy-start | bytes 393220
  181.6 63.1 %copy-start.8 = (f32[2048]{0:T(1024)S(1)}, f32[2048]{0:T(1024)}, u32[]{:S(2)}) copy-start(f32[2048]{0:T(1024)} %param.22) | copy-start | bytes 24580
  201.7 0.7 copy-start.6
  203.8 79.7 %all-gather.8.cloned.1.call-start = ((), (), s32[]{:S(2)}) async-start(), calls=%async_computation.5 | async-start | bytes 1179648 | tf_op jit(solution)/shard_map/all_gather | solution.py:179
  246.4 81.7 %reduce-scatter.5.cloned.1.call-start = ((), (), s32[]{:S(2)}) async-start(), calls=%async_computation.6 | async-start | bytes 1179648 | tf_op jit(solution)/shard_map/reduce_scatter | solution.py:184
  286.2 41.8 %copy-start.3 = (bf16[32,2048]{1,0:T(8,128)(2,1)S(1)}, bf16[32,2048]{1,0:T(8,128)(2,1)}, u32[]{:S(2)}) copy-start(bf16[32,2048]{1,0:T(8,128)(2,1)} %reduce-scatter.3.cloned.1.call-done) | copy-start | bytes 393220
  290.5 38.8 %copy-start.9 = (f32[2048]{0:T(1024)S(1)}, f32[2048]{0:T(1024)}, u32[]{:S(2)}) copy-start(f32[2048]{0:T(1024)} %param.26) | copy-start | bytes 24580
  329.1 0.7 copy-start.5
  329.8 7.4 %collective-permute-start = (bf16[32,2048]{1,0:T(8,128)(2,1)S(1)}, bf16[32,2048]{1,0:T(8,128)(2,1)}, u32[]{:S(2)}, u32[]{:S(2)}) collective-permute-start(bf16[32,2048]{1,0:T(8,128)(2,1)S(1)} %get-tuple-element.25), channel_id=1, source_target_pairs={{0,32},{32,64},{64,96},{96,128},{128,160},{160,192},{192,224},{224... | collective-permute-start | bytes 393224 | tf_op jit(solution)/shard_map/ppermute | solution.py:19
  330.7 6.5 %collective-permute-start.1 = (bf16[32,2048]{1,0:T(8,128)(2,1)S(1)}, bf16[32,2048]{1,0:T(8,128)(2,1)}, u32[]{:S(2)}, u32[]{:S(2)}) collective-permute-start(bf16[32,2048]{1,0:T(8,128)(2,1)S(1)} %get-tuple-element.25), channel_id=1, source_target_pairs={{0,224},{32,0},{64,32},{96,64},{128,96},{160,128},{192,160},{224,1... | collective-permute-start | bytes 393224 | tf_op jit(solution)/shard_map/ppermute | solution.py:22
  337.2 6.7 %collective-permute-start.2 = (bf16[32,2048]{1,0:T(8,128)(2,1)}, bf16[32,2048]{1,0:T(8,128)(2,1)S(1)}, u32[]{:S(2)}, u32[]{:S(2)}) collective-permute-start(bf16[32,2048]{1,0:T(8,128)(2,1)} %collective-permute-done), channel_id=1, source_target_pairs={{0,32},{32,64},{64,96},{96,128},{128,160},{160,192},{192,224},{224... | collective-permute-start | bytes 393224 | tf_op jit(solution)/shard_map/ppermute | solution.py:19
  337.2 6.7 %collective-permute-start.3 = (bf16[32,2048]{1,0:T(8,128)(2,1)}, bf16[32,2048]{1,0:T(8,128)(2,1)S(1)}, u32[]{:S(2)}, u32[]{:S(2)}) collective-permute-start(bf16[32,2048]{1,0:T(8,128)(2,1)} %collective-permute-done.1), channel_id=1, source_target_pairs={{0,224},{32,0},{64,32},{96,64},{128,96},{160,128},{192,160},{224,1... | collective-permute-start | bytes 393224 | tf_op jit(solution)/shard_map/ppermute | solution.py:22
  343.9 6.2 %collective-permute-start.4 = (bf16[32,2048]{1,0:T(8,128)(2,1)S(1)}, bf16[32,2048]{1,0:T(8,128)(2,1)S(1)}, u32[]{:S(2)}, u32[]{:S(2)}) collective-permute-start(bf16[32,2048]{1,0:T(8,128)(2,1)S(1)} %collective-permute-done.2), channel_id=1, source_target_pairs={{0,32},{32,64},{64,96},{96,128},{128,160},{160,192},{192,224},{224... | collective-permute-start | bytes 393224 | tf_op jit(solution)/shard_map/ppermute | solution.py:19
  343.9 6.2 %collective-permute-start.5 = (bf16[32,2048]{1,0:T(8,128)(2,1)S(1)}, bf16[32,2048]{1,0:T(8,128)(2,1)S(1)}, u32[]{:S(2)}, u32[]{:S(2)}) collective-permute-start(bf16[32,2048]{1,0:T(8,128)(2,1)S(1)} %collective-permute-done.3), channel_id=1, source_target_pairs={{0,224},{32,0},{64,32},{96,64},{128,96},{160,128},{192,160},{224,1... | collective-permute-start | bytes 393224 | tf_op jit(solution)/shard_map/ppermute | solution.py:22
  350.1 6.2 %collective-permute-start.6 = (bf16[32,2048]{1,0:T(8,128)(2,1)S(1)}, bf16[32,2048]{1,0:T(8,128)(2,1)S(1)}, u32[]{:S(2)}, u32[]{:S(2)}) collective-permute-start(bf16[32,2048]{1,0:T(8,128)(2,1)S(1)} %collective-permute-done.4), channel_id=1, source_target_pairs={{0,32},{32,64},{64,96},{96,128},{128,160},{160,192},{192,224},{224... | collective-permute-start | bytes 393224 | tf_op jit(solution)/shard_map/ppermute | solution.py:19
Sparse Core Ops, SparseCore 0:
  11.1 60.7 all-gather.5
  74.4 84.2 all-gather.3
  204.0 39.6 reduce-scatter.2
  246.5 37.0 all-gather.7
  290.7 37.3 reduce-scatter.4
